TPU v7x, 32 devices: a whole 2x2x4 slice. The times are simulated.
32 devices in a mesh: seq: 8 (over z, y), tp: 4 (over x, core).
Axes of the slice: x: 2, y: 2, z: 4, core: 2. Of those that a mesh axis runs over, the one named last changes fastest.
Arguments:
- tokens: bfloat16 [2048, 2560], P('seq', 'tp'), may hold values from -6 to 6
- segments: int32 [8, 256], P('seq'), may hold values from 0 to 3, never falling along the last dimension, each value on 1 to 128 neighbouring positions
- routes: int32 [2048, 6], P('seq'), may hold values from 0 to 63, all different within a row; in each aligned block of 256 rows (0 to 255, 256 to 511, ...) at most 40 rows name the same one
- page_table: int32 [8, 32], P('seq'), may hold values from 0 to 31, each once within a row
- cache_pool: bfloat16 [256, 16, 1024], P('seq', None, 'tp'), may hold values from -6 to 6
- attn_gain: float32 [2560], replicated, may hold values from 0.1 to 1.9
- w_query: bfloat16 [2560, 2048], P(None, 'tp'), may hold values from -0.125 to 0.125
- w_keyval: bfloat16 [2560, 1024], P(None, 'tp'), may hold values from -0.125 to 0.125
- w_out: bfloat16 [2048, 2560], P('tp'), may hold values from -0.125 to 0.125
- ffn_gain: float32 [2560], replicated, may hold values from 0.1 to 1.9
- w_router: bfloat16 [2560, 64], replicated, may hold values from -0.125 to 0.125
- expert_gate: bfloat16 [64, 1536, 2560], P('seq', 'tp'), may hold values from -0.125 to 0.125
- expert_up: bfloat16 [64, 1536, 2560], P('seq', 'tp'), may hold values from -0.125 to 0.125
- expert_down: bfloat16 [64, 1536, 2560], P('seq', 'tp'), may hold values from -0.15625 to 0.15625
- shared_gate: bfloat16 [1536, 2560], P('tp'), may hold values from -0.125 to 0.125
- shared_up: bfloat16 [1536, 2560], P('tp'), may hold values from -0.125 to 0.125
- shared_down: bfloat16 [1536, 2560], P('tp'), may hold values from -0.15625 to 0.15625
Outputs:
- layer_out: bfloat16 [2048, 2560], P('seq', 'tp')
- cache_out: bfloat16 [256, 16, 1024], P('seq', None, 'tp')
Inputs may be any that keep to these rules, and one draw needn't show every extreme that they name: `segments`: each row is one worker's block; ids never fall along a row, every segment has 1 to 128 slots and one has exactly 128. `routes`: within the 256 tokens of one worker no expert is named more than 40 times, a bound that some block reaches. `page_table`: each row lists every page of one worker's pool once; its first 16 entries take the worker's blocks in order.
All inputs are finite; a program needn't handle non-finite values.
Results may differ from a plain program's by a relative error of at most 0.019.
Values may be sent and summed in bfloat16 or wider, within the bound.
A program may use at most 192 MiB of HBM per device.

v0:
```python
import jax
import jax.numpy as jnp
from jax import lax
from jax.sharding import PartitionSpec as P

HEAD = 128
PAGE = 16
norm_eps = 1e-05
rope_base = 500000.0


def partner(block, axis, distance):
    count = lax.axis_size(axis)
    route = []
    for low in range(count):
        high = low | 1 << distance
        if high != low and high < count:
            route += [(low, high), (high, low)]
    return lax.ppermute(block, axis, route)


def gather_all(block):
    return lax.all_gather(block, ("seq", "tp"), axis=0)


def scatter_all(whole):
    part = lax.psum_scatter(whole, "tp", scatter_dimension=2, tiled=True)
    return lax.psum_scatter(part, "seq", scatter_dimension=0, tiled=False)


def rms_scale(inputs, gain_vec):
    return (
        inputs * lax.rsqrt(jnp.mean(inputs * inputs, axis=-1, keepdims=True) + norm_eps) * gain_vec
    )


def in_segment(segment_row):
    row_order = jnp.arange(segment_row.shape[0], dtype=jnp.int32)
    before = (segment_row[:, None] == segment_row[None, :]) & (
        row_order[None, :] < row_order[:, None]
    )
    return jnp.sum(before.astype(jnp.int32), axis=1)


def rotate(inputs, position):
    half_size = inputs.shape[-1] // 2
    inv_freq = rope_base ** (-jnp.arange(half_size, dtype=jnp.float32) * 2.0 / inputs.shape[-1])
    angles = position.astype(jnp.float32)[:, None] * inv_freq[None, :]
    cosine = jnp.cos(angles)[:, None, :]
    sine_term = jnp.sin(angles)[:, None, :]
    leading = inputs[..., :half_size]
    trailing = inputs[..., half_size:]
    return jnp.concatenate(
        [leading * cosine - trailing * sine_term, trailing * cosine + leading * sine_term], axis=-1
    )


def shards(
    tokens,
    segments,
    routes,
    page_table,
    cache_pool,
    attn_gain,
    w_query,
    w_keyval,
    w_out,
    ffn_gain,
    w_router,
    expert_gate,
    expert_up,
    expert_down,
    shared_gate,
    shared_up,
    shared_down,
):
    tp_count = lax.axis_size("tp")
    seq_count = lax.axis_size("seq")
    tp_rank = lax.axis_index("tp")
    row_count = tokens.shape[0]
    col_width = tokens.shape[1]
    model_width = col_width * tp_count
    whole_rows = lax.all_gather(tokens, "tp", axis=1, tiled=True)
    residual = whole_rows.astype(jnp.float32)
    normed_in = rms_scale(residual, attn_gain).astype(jnp.bfloat16)
    segment_row = segments[0]
    position = in_segment(segment_row)
    local_heads = w_query.shape[1] // HEAD
    queries = jnp.dot(normed_in, w_query, preferred_element_type=jnp.float32).reshape(
        row_count, local_heads, HEAD
    )
    queries = rotate(queries, position).astype(jnp.bfloat16)
    keyval = jnp.dot(normed_in, w_keyval, preferred_element_type=jnp.float32)
    if w_keyval.shape[1] == HEAD:
        is_key = tp_rank % 2 == 0
        rotated = rotate(keyval.reshape(row_count, 1, HEAD), position).reshape(row_count, HEAD)
        own_half = jnp.where(is_key, rotated, keyval).astype(jnp.bfloat16)
        other_half = partner(own_half, "tp", 0)
        key_rows = jnp.where(is_key, own_half, other_half)
        values = jnp.where(is_key, other_half, own_half)
        cache_rows = own_half
    else:
        key_rows = (
            rotate(keyval[:, :HEAD].reshape(row_count, 1, HEAD), position)
            .reshape(row_count, HEAD)
            .astype(jnp.bfloat16)
        )
        values = keyval[:, HEAD:].astype(jnp.bfloat16)
        cache_rows = jnp.concatenate([key_rows, values], axis=1)
    scores = jnp.einsum(
        "qhd,kd->hqk", queries, key_rows, preferred_element_type=jnp.float32
    ) * HEAD ** (-0.5)
    row_order = jnp.arange(row_count, dtype=jnp.int32)
    allowed = (segment_row[:, None] == segment_row[None, :]) & (
        row_order[None, :] <= row_order[:, None]
    )
    weights = jnp.where(allowed[None], jnp.exp(scores), 0.0)
    attn_probs = (weights / jnp.sum(weights, axis=-1, keepdims=True)).astype(jnp.bfloat16)
    attended = jnp.einsum("hqk,kd->qhd", attn_probs, values, preferred_element_type=jnp.float32)
    attended = attended.astype(jnp.bfloat16).reshape(row_count, local_heads * HEAD)
    attn_part = jnp.dot(attended, w_out, preferred_element_type=jnp.float32)
    attn_mine = lax.psum_scatter(
        attn_part.astype(jnp.bfloat16), "tp", scatter_dimension=1, tiled=True
    )
    hidden_mine = tokens.astype(jnp.float32) + attn_mine.astype(jnp.float32)
    seq_rank = lax.axis_index("seq")
    gathered = gather_all(hidden_mine.astype(jnp.bfloat16))
    hidden_all = (
        gathered.reshape(seq_count, tp_count, row_count, col_width)
        .transpose(0, 2, 1, 3)
        .reshape(seq_count, row_count, model_width)
    )
    normed_all = rms_scale(hidden_all.astype(jnp.float32), ffn_gain).astype(jnp.bfloat16)
    top_count = routes.shape[1]
    local_experts = expert_gate.shape[0]
    expert_total = local_experts * seq_count
    capacity = (
        (row_count * top_count * 5 // (expert_total * 3) + tp_count - 1) // tp_count * tp_count
    )
    slots = local_experts * capacity
    routes_all = lax.all_gather(routes, "seq", axis=0)
    chosen = jnp.sum(
        (routes_all[:, :, :, None] == jnp.arange(expert_total, dtype=jnp.int32)).astype(
            jnp.float32
        ),
        axis=2,
    )
    logits = jnp.einsum("wtd,de->wte", normed_all, w_router, preferred_element_type=jnp.float32)
    lifted = jnp.where(chosen > 0, jnp.exp(logits), 0.0)
    route_weight = lifted / jnp.sum(lifted, axis=2, keepdims=True)
    first = seq_rank * local_experts
    named = lax.dynamic_slice_in_dim(chosen, first, local_experts, 2)
    weight_mine = lax.dynamic_slice_in_dim(route_weight, first, local_experts, 2)
    earlier = (row_order[:, None] > row_order[None, :]).astype(jnp.bfloat16)
    rank = jnp.einsum(
        "ts,wse->wte", earlier, named.astype(jnp.bfloat16), preferred_element_type=jnp.float32
    ).astype(jnp.int32)
    place = jnp.where(named > 0, rank, -1)
    hit = (
        place.transpose(0, 2, 1)[:, :, None, :]
        == jnp.arange(capacity, dtype=jnp.int32)[None, None, :, None]
    )
    select = hit.astype(jnp.bfloat16).reshape(seq_count, slots, row_count)
    slot_weight = jnp.sum(
        jnp.where(hit, weight_mine.transpose(0, 2, 1)[:, :, None, :], 0.0), axis=3
    )
    slot_rows = (
        jnp.einsum("wst,wtd->wsd", select, normed_all, preferred_element_type=jnp.float32)
        .astype(jnp.bfloat16)
        .reshape(seq_count, local_experts, capacity, model_width)
    )
    gate_out = jnp.einsum(
        "secd,efd->secf", slot_rows, expert_gate, preferred_element_type=jnp.float32
    )
    up_out = jnp.einsum("secd,efd->secf", slot_rows, expert_up, preferred_element_type=jnp.float32)
    activation = (jax.nn.silu(gate_out) * up_out * slot_weight[..., None]).astype(jnp.bfloat16)
    group_part = (
        jnp.einsum("secf,efd->secd", activation, expert_down, preferred_element_type=jnp.float32)
        .astype(jnp.bfloat16)
        .reshape(seq_count, slots, model_width)
    )
    normed_mid = lax.dynamic_index_in_dim(normed_all, seq_rank, 0, keepdims=False)
    shared_gate_out = jnp.einsum(
        "td,fd->tf", normed_mid, shared_gate, preferred_element_type=jnp.float32
    )
    shared_up_out = jnp.einsum(
        "td,fd->tf", normed_mid, shared_up, preferred_element_type=jnp.float32
    )
    shared_act = (jax.nn.silu(shared_gate_out) * shared_up_out).astype(jnp.bfloat16)
    shared_part = jnp.dot(shared_act, shared_down, preferred_element_type=jnp.float32)
    routed_part = jnp.einsum("wst,wsd->wtd", select, group_part, preferred_element_type=jnp.float32)
    is_mine = jnp.arange(seq_count, dtype=jnp.int32)[:, None, None] == seq_rank
    summand = routed_part + jnp.where(is_mine, shared_part[None], 0.0)
    output_share = scatter_all(summand.astype(jnp.bfloat16)).astype(jnp.float32)
    layer_out = (hidden_mine + output_share).astype(jnp.bfloat16)
    page_count = row_count // PAGE
    new_pages = cache_rows.reshape(page_count, PAGE, cache_rows.shape[1])
    cache_out = cache_pool.at[page_table[0, :page_count]].set(new_pages)
    return (layer_out, cache_out)


def solution(mesh):
    in_specs = (
        P("seq", "tp"),
        P("seq", None),
        P("seq", None),
        P("seq", None),
        P("seq", None, "tp"),
        P(),
        P(None, "tp"),
        P(None, "tp"),
        P("tp", None),
        P(),
        P(),
        P("seq", "tp", None),
        P("seq", "tp", None),
        P("seq", "tp", None),
        P("tp", None),
        P("tp", None),
        P("tp", None),
    )
    out_specs = (P("seq", "tp"), P("seq", None, "tp"))
    return jax.shard_map(shards, mesh=mesh, in_specs=in_specs, out_specs=out_specs, check_vma=False)
```

profile of v0, /device:TPU:0, one launch (start us, length us, event | category | flops | bytes accessed | tf_op | source)
XLA Modules:
  0.0 479.4 jit_solution(7024119431726332237)
XLA Ops:
  10.3 20.2 %all-gather.5.cloned.1.call-done = bf16[256,2560]{1,0:T(8,128)(2,1)} async-done(((bf16[256,640]{1,0:T(8,128)(2,1)}), bf16[256,2560]{1,0:T(8,128)(2,1)}) %all-gather.5.cloned.1.call-update) | async-done | bytes 1310736 | tf_op jit(solution)/shard_map/all_gather | solution.py:83
  30.5 1.7 fusion.15
  32.2 3.9 fusion.56
  36.0 1.2 reshape.242
  37.2 2.5 fusion.58
  40.7 1.4 fusion.24
  42.1 1.9 convolution_convert_fusion.2
  44.1 2.0 convolution_convert_fusion.1
  46.0 2.4 copy.76
  48.5 26.6 %reduce-scatter.10.cloned.1.call-done = bf16[640,256]{1,0:T(8,128)(2,1)} async-done(((bf16[2560,256]{1,0:T(8,128)(2,1)}), bf16[640,256]{1,0:T(8,128)(2,1)}) %reduce-scatter.10.cloned.1.call-update) | async-done | bytes 327696
  77.3 30.6 %all-gather = s32[2048,6]{0,1:T(8,128)S(1)} all-gather(s32[256,6]{0,1:T(8,128)S(1)} %copy-done.13), channel_id=2, replica_groups=mesh['seq'=8,'tp'=4] {'seq'}, dimensions={0}, use_global_device_ids=true | all-gather | bytes 55296 | tf_op jit(solution)/shard_map/all_gather | solution.py:141
  109.1 56.6 %all-gather.7.cloned.1.call-done = bf16[8192,640]{1,0:T(8,128)(2,1)} async-done(((bf16[256,640]{1,0:T(8,128)(2,1)}), bf16[8192,640]{1,0:T(8,128)(2,1)}) %all-gather.7.cloned.1.call-update) | async-done | bytes 10485776 | tf_op jit(solution)/shard_map/all_gather | solution.py:23
  165.7 6.1 %multiply_reduce_fusion = f32[8192]{0:T(1024)S(1)} fusion(bf16[8192,640]{1,0:T(8,128)(2,1)} %all-gather.7.cloned.1.call-done), kind=kLoop, calls=%fused_computation.1 | loop fusion | flops 15720448 | bytes 10518528 | tf_op jit(solution)/shard_map/reduce_sum | solution.py:33
  171.9 13.8 %copy.83 = f32[8,4,32,8,640]{4,3,1,2,0:T(8,128)} copy(bf16[8,4,32,8,640]{4,3,2,1,0:T(8,128)(2,1)} %bitcast.139) | data formatting | bytes 31457280 | tf_op jit(solution)/shard_map/convert_element_type | solution.py:133
  185.7 8.4 %multiply_convert_fusion = bf16[8,256,2560]{2,1,0:T(8,128)(2,1)S(1)} fusion(f32[8,256,2560]{2,1,0:T(8,128)} %bitcast.136, f32[2560]{0:T(1024)S(1)} %copy-done.12, f32[8,256]{1,0:T(8,128)S(1)} %add_rsqrt_fusion), kind=kLoop, calls=%fused_computation.3 | loop fusion | flops 15728640 | bytes 31475712 | tf_op jit(solution)/shard_map/convert_element_type | solution.py:133
  194.1 3.3 fusion.89
  198.5 10.5 %convolution_convert_fusion = bf16[8,320,2560]{2,1,0:T(8,128)(2,1)} fusion(pred[8,320,256]{2,1,0:T(32,128)(4,1)S(1)} %bitcast_compare_fusion, bf16[8,256,2560]{2,1,0:T(8,128)(2,1)} %copy-done.2), kind=kOutput, calls=%fused_computation.13 | convolution fusion | flops 3361996800 | bytes 24248320 | tf_op jit(solution)/shard_map/wst,wtd->wsd/dot_general | solution.py:168
  209.1 14.1 %fusion.2 = f32[8,8,40,384]{3,2,1,0:T(8,128)} fusion(bf16[8,384,2560]{2,1,0:T(8,128)(2,1)} %param.29, bf16[8,8,40,2560]{3,2,1,0:T(8,128)(2,1)} %bitcast.140), kind=kOutput, calls=%fused_computation.6 | convolution fusion | flops 5033164800 | bytes 32768000 | tf_op jit(solution)/shard_map/secd,efd->secf/dot_general | solution.py:175
  223.1 24.0 %convert_bitcast_fusion = bf16[8,8,40,2560]{3,2,0,1:T(8,128)(2,1)} fusion(bf16[8,384,2560]{2,1,0:T(8,128)(2,1)} %param.30, f32[8,8,40,384]{3,2,1,0:T(8,128)} %fusion.2, bf16[8,384,2560]{2,1,0:T(8,128)(2,1)} %param.28, bf16[8,8,40,2560]{3,2,1,0:T(8,128)(2,1)} %bitcast.141, f32[8,8,40]{2,0,1:T(8,128)S(1)} %copy.67), kind=kOutput, calls=%fused_computation.10 | convolution fusion | flops 10079764480 | bytes 61614080 | tf_op jit(solution)/shard_map/secf,efd->secd/dot_general | solution.py:178
  247.2 12.5 %copy.68 = bf16[8,8,40,2560]{3,2,1,0:T(8,128)(2,1)} copy(bf16[8,8,40,2560]{3,2,0,1:T(8,128)(2,1)} %convert_bitcast_fusion) | data formatting | bytes 26214400 | tf_op jit(solution)/shard_map/convert_element_type | solution.py:179
  259.6 2.9 fusion.31
  262.6 4.3 fusion.43
  266.9 13.5 %add_convert_fusion = bf16[8,256,2560]{2,1,0:T(8,128)(2,1)} fusion(f32[256,2560]{1,0:T(8,128)S(1)} %fusion.43, pred[8]{0:T(512)(128)(4,1)S(1)} %iota_compare_fusion.5, pred[8,320,256]{2,1,0:T(32,128)(4,1)} %copy-done.4, bf16[8,320,2560]{2,1,0:T(8,128)(2,1)} %bitcast.142), kind=kOutput, calls=%fused_computation.2 | convolution fusion | flops 3371171840 | bytes 26869768 | tf_op jit(solution)/shard_map/wst,wsd->wtd/dot_general | solution.py:191
  280.4 14.7 %copy.78 = bf16[8,256,2560]{1,0,2:T(8,128)(2,1)} copy(bf16[8,256,2560]{2,1,0:T(8,128)(2,1)} %add_convert_fusion) | data formatting | bytes 20971520
  295.0 12.4 %copy.84 = bf16[320,8,8,256]{3,1,2,0:T(8,128)(2,1)} copy(bf16[320,8,8,256]{3,2,1,0:T(8,128)(2,1)} %bitcast.138) | data formatting | bytes 20971520
  307.5 83.9 %reduce-scatter.12.cloned.1.call-done = bf16[640,2048]{1,0:T(8,128)(2,1)} async-done(((bf16[2560,2048]{1,0:T(8,128)(2,1)}), bf16[640,2048]{1,0:T(8,128)(2,1)}) %reduce-scatter.12.cloned.1.call-update) | async-done | bytes 2621456
  391.4 4.1 copy.85
  395.6 5.0 %copy.79 = bf16[8,256,640]{2,1,0:T(8,128)(2,1)} copy(bf16[8,256,640]{1,0,2:T(8,128)(2,1)} %bitcast.143) | data formatting | bytes 5242880
  403.0 1.7 copy.69
  404.6 1.7 scatter_fusion
  406.4 64.7 %reduce-scatter.8.cloned.1.call-done = bf16[1,256,640]{2,1,0:T(8,128)(2,1)} async-done(((bf16[8,256,640]{2,1,0:T(8,128)(2,1)}), bf16[1,256,640]{2,1,0:T(8,128)(2,1)}) %reduce-scatter.8.cloned.1.call-update) | async-done | bytes 327696 | tf_op jit(solution)/shard_map/reduce_scatter | solution.py:28
  471.1 1.8 fusion.48
  (70 shorter events, 10.9 us)
Async XLA Ops:
  7.2 36.9 %copy-start = (bf16[512,2560]{1,0:T(8,128)(2,1)S(1)}, bf16[512,2560]{1,0:T(8,128)(2,1)}, u32[]{:S(2)}) copy-start(bf16[512,2560]{1,0:T(8,128)(2,1)} %param.25) | copy-start | bytes 7864324
  7.2 23.3 %all-gather.5.cloned.1.call-start = ((), (), s32[]{:S(2)}) async-start(), calls=%async_computation.3 | async-start | bytes 1638400 | tf_op jit(solution)/shard_map/all_gather | solution.py:83
  7.9 67.3 %reduce-scatter.10.cloned.1.call-start = ((), (), s32[]{:S(2)}) async-start(), calls=%async_computation.6 | async-start | bytes 1638400
  10.3 27.0 %copy-start.14 = (f32[2560]{0:T(1024)S(1)}, f32[2560]{0:T(1024)}, u32[]{:S(2)}) copy-start(f32[2560]{0:T(1024)} %param.22) | copy-start | bytes 30724
  39.7 0.9 copy-start.11
  40.1 0.6 copy-start.9
  40.1 0.6 copy-start.10
  44.1 32.3 %copy-start.3 = (bf16[256,640]{1,0:T(8,128)(2,1)S(1)}, bf16[256,640]{1,0:T(8,128)(2,1)}, u32[]{:S(2)}) copy-start(bf16[256,640]{1,0:T(8,128)(2,1)} %param.17) | copy-start | bytes 983044
  46.0 31.3 %copy-start.13 = (s32[256,6]{0,1:T(8,128)S(1)}, s32[256,6]{0,1:T(8,128)}, u32[]{:S(2)}) copy-start(s32[256,6]{0,1:T(8,128)} %param.19) | copy-start | bytes 18436
  48.5 117.2 %all-gather.7.cloned.1.call-start = ((), (), s32[]{:S(2)}) async-start(), calls=%async_computation.5 | async-start | bytes 10813440 | tf_op jit(solution)/shard_map/all_gather | solution.py:23
  77.2 314.3 %reduce-scatter.12.cloned.1.call-start = ((), (), s32[]{:S(2)}) async-start(), calls=%async_computation.7 | async-start | bytes 13107200
  109.0 89.5 %copy-start.4 = (pred[8,320,256]{2,1,0:T(32,128)(4,1)}, pred[8,320,256]{2,1,0:T(32,128)(4,1)S(1)}, u32[]{:S(2)}) copy-start(pred[8,320,256]{2,1,0:T(32,128)(4,1)S(1)} %bitcast_compare_fusion) | copy-start | bytes 1966084
  171.9 13.8 %copy-start.12 = (f32[2560]{0:T(1024)S(1)}, f32[2560]{0:T(1024)}, u32[]{:S(2)}) copy-start(f32[2560]{0:T(1024)} %param.26) | copy-start | bytes 30724
  185.6 8.4 %copy-start.8 = (bf16[2560,64]{0,1:T(8,128)(2,1)S(1)}, bf16[2560,64]{0,1:T(8,128)(2,1)}, u32[]{:S(2)}) copy-start(bf16[2560,64]{0,1:T(8,128)(2,1)} %param.27) | copy-start | bytes 983044
  194.0 3.9 copy-start.2
  247.2 12.5 %copy-start.5 = (bf16[384,2560]{1,0:T(8,128)(2,1)S(1)}, bf16[384,2560]{1,0:T(8,128)(2,1)}, u32[]{:S(2)}) copy-start(bf16[384,2560]{1,0:T(8,128)(2,1)} %param.31) | copy-start | bytes 5898244
  307.5 163.6 %reduce-scatter.8.cloned.1.call-start = ((), (), s32[]{:S(2)}) async-start(), calls=%async_computation.4 | async-start | bytes 2949120 | tf_op jit(solution)/shard_map/reduce_scatter | solution.py:28
  395.6 77.3 %copy-start.1 = (bf16[512,2560]{1,0:T(8,128)(2,1)S(1)}, bf16[512,2560]{1,0:T(8,128)(2,1)}, u32[]{:S(2)}) copy-start(bf16[512,2560]{1,0:T(8,128)(2,1)} %param.25) | copy-start | bytes 7864324
  395.6 5.0 %copy-start.15 = (s32[1,32]{1,0:T(1,128)S(1)}, s32[1,32]{1,0:T(1,128)}, u32[]{:S(2)}) copy-start(s32[1,32]{1,0:T(1,128)} %param.20) | copy-start | bytes 388
  395.6 9.1 %copy-start.7 = (bf16[32,16,256]{2,1,0:T(8,128)(2,1)S(1)}, bf16[32,16,256]{2,1,0:T(8,128)(2,1)}, u32[]{:S(2)}) copy-start(bf16[32,16,256]{2,1,0:T(8,128)(2,1)} %param.21) | copy-start | bytes 786436
  406.3 66.6 %copy-start.6 = (bf16[32,16,256]{2,1,0:T(8,128)(2,1)}, bf16[32,16,256]{2,1,0:T(8,128)(2,1)S(1)}, u32[]{:S(2)}) copy-start(bf16[32,16,256]{2,1,0:T(8,128)(2,1)S(1)} %scatter_fusion) | copy-start | bytes 786436
Sparse Core Ops, SparseCore 0:
  9.6 20.8 all-gather.4
  48.6 26.5 reduce-scatter.9
  79.0 86.6 all-gather.6
  307.6 83.8 reduce-scatter.11
  400.7 70.3 reduce-scatter.7
where the time goes:
time: 481 us; the launch traced here: 479 us
  waiting for transfers between devices  253 us (53%)
  matrix products  84.5 us (18%)
  local copies, waits for them, and re-layouts  72.8 us (15%)
  blocking collectives  30.6 us (6%)
  other arithmetic  24.3 us (5%)
  between operations  14.1 us (3%)
    unnamed x7, waiting for transfers between devices  111 us
    reduce_scatter x1, waiting for transfers between devices, scatter_all(): return lax.psum_scatter(part, 'seq', scatter_dimension=0, tiled=False)  64.7 us
    all_gather x1, waiting for transfers between devices, gather_all(): return lax.all_gather(block, ('seq', 'tp'), axis=0)  56.6 us
    unnamed x38, local copies, waits for them, and re-layouts  40.6 us
    all_gather x1, blocking collectives, shards(): routes_all = lax.all_gather(routes, 'seq', axis=0)  30.6 us
    dot_general x1, matrix products, shards(): jnp.einsum('secf,efd->secd', activation, expert_down, preferred_element_t...  24 us
    all_gather x1, waiting for transfers between devices, shards(): whole_rows = lax.all_gather(tokens, 'tp', axis=1, tiled=True)  20.2 us
    dot_general x1, matrix products, shards(): jnp.einsum('secd,efd->secf', slot_rows, expert_up, preferred_element_type...  14.1 us
  transfers between devices with their start and end apart: 5, of which 5 were waited for; matrix products, arithmetic and copies ran while one was open for 2% of the time, Pallas kernels for 0%

commit v1 on v0

--- a/solution.py
+++ b/solution.py
@@ -80,7 +80,9 @@
     row_count = tokens.shape[0]
     col_width = tokens.shape[1]
     model_width = col_width * tp_count
-    whole_rows = lax.all_gather(tokens, "tp", axis=1, tiled=True)
+    whole_rows = jnp.concatenate(
+        lax.all_to_all(jnp.stack([tokens] * lax.axis_size("tp")), "tp", 0, 0), axis=1
+    )
     residual = whole_rows.astype(jnp.float32)
     normed_in = rms_scale(residual, attn_gain).astype(jnp.bfloat16)
     segment_row = segments[0]

time: 481 us -> 481 us (level)
  local copies, waits for them, and re-layouts: 72.8 us -> 80.6 us
  waiting for transfers between devices: 253 us -> 246 us
  matrix products: 84.5 us -> 79.5 us
    all_gather x1 -> x0, waiting for transfers between devices: 20.2 us -> none  [shards(): whole_rows = lax.all_gather(tokens, 'tp', axis=1, tiled=True)]
    all_to_all x0 -> x1, waiting for transfers between devices: none -> 12.9 us  [shards(): lax.all_to_all(jnp.stack([tokens] * lax.axis_size('tp')), 'tp', 0, 0)]
    unnamed x7 -> x6, waiting for transfers between devices: 111 us -> 112 us
    unnamed x38 -> x46, local copies, waits for them, and re-layouts: 40.6 us -> 40.9 us
where the time goes in v1:
time: 481 us; the launch traced here: 480 us
  waiting for transfers between devices  246 us (51%)
  local copies, waits for them, and re-layouts  80.6 us (17%)
  matrix products  79.5 us (17%)
  blocking collectives  30.6 us (6%)
  other arithmetic  24.9 us (5%)
  between operations  14.2 us (3%)
    unnamed x6, waiting for transfers between devices  112 us
    reduce_scatter x1, waiting for transfers between devices, scatter_all(): return lax.psum_scatter(part, 'seq', scatter_dimension=0, tiled=False)  64.7 us
    all_gather x1, waiting for transfers between devices, gather_all(): return lax.all_gather(block, ('seq', 'tp'), axis=0)  56.6 us
    unnamed x46, local copies, waits for them, and re-layouts  40.9 us
    all_gather x1, blocking collectives, shards(): routes_all = lax.all_gather(routes, 'seq', axis=0)  30.6 us
    dot_general x1, matrix products, shards(): jnp.einsum('secf,efd->secd', activation, expert_down, preferred_element_t...  24 us
    dot_general x1, matrix products, shards(): jnp.einsum('secd,efd->secf', slot_rows, expert_up, preferred_element_type...  14.1 us
    convert_element_type x1, local copies, waits for them, and re-layouts, shards(): hidden_all.astype(jnp.float32)  13.8 us
  transfers between devices with their start and end apart: 5, of which 5 were waited for; matrix products, arithmetic and copies ran while one was open for 2% of the time, Pallas kernels for 0%

profile of v1, /device:TPU:0, one launch (start us, length us, event | category | flops | bytes accessed | tf_op | source)
XLA Modules:
  0.0 480.1 jit_solution(12940045814083251972)
XLA Ops:
  7.2 2.3 stack.2
  9.5 4.3 all-to-all-start
  14.0 4.4 copy.96
  18.8 12.9 %all-to-all-done = bf16[4,256,640]{2,1,0:T(8,128)(2,1)} async-done(((bf16[4,256,640]{2,1,0:T(8,128)(2,1)}), bf16[4,256,640]{2,1,0:T(8,128)(2,1)}, u32[]{:S(2)}, u32[]{:S(2)}) %all-to-all-start) | async-done | bytes 1310752 | tf_op jit(solution)/shard_map/all_to_all | solution.py:84
  31.7 2.4 copy.73
  34.2 1.8 multiply_reduce_fusion.1
  36.0 1.7 fusion.16
  41.8 1.9 convolution_convert_fusion.2
  43.7 1.9 convolution_convert_fusion.1
  45.7 2.5 copy.97
  48.2 27.8 %reduce-scatter.10.cloned.1.call-done = bf16[640,256]{1,0:T(8,128)(2,1)} async-done(((bf16[2560,256]{1,0:T(8,128)(2,1)}), bf16[640,256]{1,0:T(8,128)(2,1)}) %reduce-scatter.10.cloned.1.call-update) | async-done | bytes 327696
  78.1 30.6 %all-gather = s32[2048,6]{0,1:T(8,128)S(1)} all-gather(s32[256,6]{0,1:T(8,128)S(1)} %copy-done.17), channel_id=2, replica_groups=mesh['seq'=8,'tp'=4] {'seq'}, dimensions={0}, use_global_device_ids=true | all-gather | bytes 55296 | tf_op jit(solution)/shard_map/all_gather | solution.py:143
  109.9 56.6 %all-gather.4.cloned.1.call-done = bf16[8192,640]{1,0:T(8,128)(2,1)} async-done(((bf16[256,640]{1,0:T(8,128)(2,1)}), bf16[8192,640]{1,0:T(8,128)(2,1)}) %all-gather.4.cloned.1.call-update) | async-done | bytes 10485776 | tf_op jit(solution)/shard_map/all_gather | solution.py:23
  166.4 6.1 %multiply_reduce_fusion = f32[8192]{0:T(1024)S(1)} fusion(bf16[8192,640]{1,0:T(8,128)(2,1)} %all-gather.4.cloned.1.call-done), kind=kLoop, calls=%fused_computation.1 | loop fusion | flops 15720448 | bytes 10518528 | tf_op jit(solution)/shard_map/reduce_sum | solution.py:33
  172.6 13.8 %copy.102 = f32[8,4,32,8,640]{4,3,1,2,0:T(8,128)} copy(bf16[8,4,32,8,640]{4,3,2,1,0:T(8,128)(2,1)} %bitcast.156) | data formatting | bytes 31457280 | tf_op jit(solution)/shard_map/convert_element_type | solution.py:135
  186.4 8.4 %multiply_convert_fusion = bf16[8,256,2560]{2,1,0:T(8,128)(2,1)S(1)} fusion(f32[8,256,2560]{2,1,0:T(8,128)} %bitcast.153, f32[2560]{0:T(1024)S(1)} %copy-done.16, f32[8,256]{1,0:T(8,128)S(1)} %add_rsqrt_fusion), kind=kLoop, calls=%fused_computation.3 | loop fusion | flops 15728640 | bytes 31475712 | tf_op jit(solution)/shard_map/convert_element_type | solution.py:135
  194.8 3.3 fusion.83
  199.2 10.5 %convolution_convert_fusion = bf16[8,320,2560]{2,1,0:T(8,128)(2,1)} fusion(pred[8,320,256]{2,1,0:T(32,128)(4,1)S(1)} %bitcast_compare_fusion, bf16[8,256,2560]{2,1,0:T(8,128)(2,1)} %copy-done.2), kind=kOutput, calls=%fused_computation.13 | convolution fusion | flops 3361996800 | bytes 24248320 | tf_op jit(solution)/shard_map/wst,wtd->wsd/dot_general | solution.py:170
  209.8 14.1 %fusion.2 = f32[8,8,40,384]{3,2,1,0:T(8,128)} fusion(bf16[8,384,2560]{2,1,0:T(8,128)(2,1)} %param.29, bf16[8,8,40,2560]{3,2,1,0:T(8,128)(2,1)} %bitcast.157), kind=kOutput, calls=%fused_computation.6 | convolution fusion | flops 5033164800 | bytes 32768000 | tf_op jit(solution)/shard_map/secd,efd->secf/dot_general | solution.py:177
  223.9 24.0 %convert_bitcast_fusion = bf16[8,8,40,2560]{3,2,0,1:T(8,128)(2,1)} fusion(bf16[8,384,2560]{2,1,0:T(8,128)(2,1)} %param.30, f32[8,8,40,384]{3,2,1,0:T(8,128)} %fusion.2, bf16[8,384,2560]{2,1,0:T(8,128)(2,1)} %param.28, bf16[8,8,40,2560]{3,2,1,0:T(8,128)(2,1)} %bitcast.158, f32[8,8,40]{2,0,1:T(8,128)S(1)} %copy.84), kind=kOutput, calls=%fused_computation.10 | convolution fusion | flops 10079764480 | bytes 61614080 | tf_op jit(solution)/shard_map/secf,efd->secd/dot_general | solution.py:180
  247.9 12.5 %copy.85 = bf16[8,8,40,2560]{3,2,1,0:T(8,128)(2,1)} copy(bf16[8,8,40,2560]{3,2,0,1:T(8,128)(2,1)} %convert_bitcast_fusion) | data formatting | bytes 26214400 | tf_op jit(solution)/shard_map/convert_element_type | solution.py:181
  260.4 2.9 fusion.30
  263.3 4.3 fusion.42
  267.6 13.5 %add_convert_fusion = bf16[8,256,2560]{2,1,0:T(8,128)(2,1)} fusion(f32[256,2560]{1,0:T(8,128)S(1)} %fusion.42, pred[8]{0:T(512)(128)(4,1)S(1)} %iota_compare_fusion.5, pred[8,320,256]{2,1,0:T(32,128)(4,1)} %copy-done.6, bf16[8,320,2560]{2,1,0:T(8,128)(2,1)} %bitcast.159), kind=kOutput, calls=%fused_computation.2 | convolution fusion | flops 3371171840 | bytes 26869768 | tf_op jit(solution)/shard_map/wst,wsd->wtd/dot_general | solution.py:193
  281.1 14.7 %copy.99 = bf16[8,256,2560]{1,0,2:T(8,128)(2,1)} copy(bf16[8,256,2560]{2,1,0:T(8,128)(2,1)} %add_convert_fusion) | data formatting | bytes 20971520
  295.8 12.4 %copy.103 = bf16[320,8,8,256]{3,1,2,0:T(8,128)(2,1)} copy(bf16[320,8,8,256]{3,2,1,0:T(8,128)(2,1)} %bitcast.155) | data formatting | bytes 20971520
  308.3 83.9 %reduce-scatter.12.cloned.1.call-done = bf16[640,2048]{1,0:T(8,128)(2,1)} async-done(((bf16[2560,2048]{1,0:T(8,128)(2,1)}), bf16[640,2048]{1,0:T(8,128)(2,1)}) %reduce-scatter.12.cloned.1.call-update) | async-done | bytes 2621456
  392.2 4.1 copy.104
  396.3 5.0 %copy.100 = bf16[8,256,640]{2,1,0:T(8,128)(2,1)} copy(bf16[8,256,640]{1,0,2:T(8,128)(2,1)} %bitcast.160) | data formatting | bytes 5242880
  405.4 1.7 scatter_fusion
  407.1 64.7 %reduce-scatter.8.cloned.1.call-done = bf16[1,256,640]{2,1,0:T(8,128)(2,1)} async-done(((bf16[8,256,640]{2,1,0:T(8,128)(2,1)}), bf16[1,256,640]{2,1,0:T(8,128)(2,1)}) %reduce-scatter.8.cloned.1.call-update) | async-done | bytes 327696 | tf_op jit(solution)/shard_map/reduce_scatter | solution.py:28
  471.8 1.8 fusion.47
  (81 shorter events, 13.1 us)
Async XLA Ops:
  7.2 36.5 %copy-start = (bf16[512,2560]{1,0:T(8,128)(2,1)S(1)}, bf16[512,2560]{1,0:T(8,128)(2,1)}, u32[]{:S(2)}) copy-start(bf16[512,2560]{1,0:T(8,128)(2,1)} %param.25) | copy-start | bytes 7864324
  7.2 6.7 %copy-start.15 = (s32[1,256]{1,0:T(1,128)S(1)}, s32[1,256]{1,0:T(1,128)}, u32[]{:S(2)}) copy-start(s32[1,256]{1,0:T(1,128)} %param.18) | copy-start | bytes 3076
  7.2 6.8 %copy-start.14 = (f32[2560]{0:T(1024)S(1)}, f32[2560]{0:T(1024)}, u32[]{:S(2)}) copy-start(f32[2560]{0:T(1024)} %param.22) | copy-start | bytes 30724
  9.5 22.2 %all-to-all-start = ((bf16[4,256,640]{2,1,0:T(8,128)(2,1)}), bf16[4,256,640]{2,1,0:T(8,128)(2,1)}, u32[]{:S(2)}, u32[]{:S(2)}) async-start(bf16[4,256,640]{2,1,0:T(8,128)(2,1)} %stack.2), calls=%async_computation | async-start | bytes 2621440 | tf_op jit(solution)/shard_map/all_to_all | solution.py:84
  13.8 62.2 %reduce-scatter.10.cloned.1.call-start = ((), (), s32[]{:S(2)}) async-start(), calls=%async_computation.6 | async-start | bytes 1638400
  34.2 3.6 copy-start.3
  34.2 4.0 copy-start.18
  37.8 1.7 copy-start.5
  38.8 3.0 copy-start.11
  39.2 1.2 copy-start.12
  39.2 1.2 copy-start.13
  45.6 31.5 %copy-start.4 = (bf16[256,640]{1,0:T(8,128)(2,1)S(1)}, bf16[256,640]{1,0:T(8,128)(2,1)}, u32[]{:S(2)}) copy-start(bf16[256,640]{1,0:T(8,128)(2,1)} %param.17) | copy-start | bytes 983044
  45.7 32.5 %copy-start.17 = (s32[256,6]{0,1:T(8,128)S(1)}, s32[256,6]{0,1:T(8,128)}, u32[]{:S(2)}) copy-start(s32[256,6]{0,1:T(8,128)} %param.19) | copy-start | bytes 18436
  48.1 118.3 %all-gather.4.cloned.1.call-start = ((), (), s32[]{:S(2)}) async-start(), calls=%async_computation.5 | async-start | bytes 10813440 | tf_op jit(solution)/shard_map/all_gather | solution.py:23
  78.0 314.2 %reduce-scatter.12.cloned.1.call-start = ((), (), s32[]{:S(2)}) async-start(), calls=%async_computation.7 | async-start | bytes 13107200
  109.8 89.4 %copy-start.6 = (pred[8,320,256]{2,1,0:T(32,128)(4,1)}, pred[8,320,256]{2,1,0:T(32,128)(4,1)S(1)}, u32[]{:S(2)}) copy-start(pred[8,320,256]{2,1,0:T(32,128)(4,1)S(1)} %bitcast_compare_fusion) | copy-start | bytes 1966084
  172.6 13.8 %copy-start.16 = (f32[2560]{0:T(1024)S(1)}, f32[2560]{0:T(1024)}, u32[]{:S(2)}) copy-start(f32[2560]{0:T(1024)} %param.26) | copy-start | bytes 30724
  186.4 8.4 %copy-start.10 = (bf16[2560,64]{0,1:T(8,128)(2,1)S(1)}, bf16[2560,64]{0,1:T(8,128)(2,1)}, u32[]{:S(2)}) copy-start(bf16[2560,64]{0,1:T(8,128)(2,1)} %param.27) | copy-start | bytes 983044
  194.8 3.9 copy-start.2
  247.9 12.5 %copy-start.7 = (bf16[384,2560]{1,0:T(8,128)(2,1)S(1)}, bf16[384,2560]{1,0:T(8,128)(2,1)}, u32[]{:S(2)}) copy-start(bf16[384,2560]{1,0:T(8,128)(2,1)} %param.31) | copy-start | bytes 5898244
  308.2 163.6 %reduce-scatter.8.cloned.1.call-start = ((), (), s32[]{:S(2)}) async-start(), calls=%async_computation.4 | async-start | bytes 2949120 | tf_op jit(solution)/shard_map/reduce_scatter | solution.py:28
  396.3 5.0 %copy-start.19 = (s32[1,32]{1,0:T(1,128)S(1)}, s32[1,32]{1,0:T(1,128)}, u32[]{:S(2)}) copy-start(s32[1,32]{1,0:T(1,128)} %param.20) | copy-start | bytes 388
  396.3 9.1 %copy-start.9 = (bf16[32,16,256]{2,1,0:T(8,128)(2,1)S(1)}, bf16[32,16,256]{2,1,0:T(8,128)(2,1)}, u32[]{:S(2)}) copy-start(bf16[32,16,256]{2,1,0:T(8,128)(2,1)} %param.21) | copy-start | bytes 786436
  396.3 77.3 %copy-start.1 = (bf16[512,2560]{1,0:T(8,128)(2,1)S(1)}, bf16[512,2560]{1,0:T(8,128)(2,1)}, u32[]{:S(2)}) copy-start(bf16[512,2560]{1,0:T(8,128)(2,1)} %param.25) | copy-start | bytes 7864324
  407.1 66.5 %copy-start.8 = (bf16[32,16,256]{2,1,0:T(8,128)(2,1)}, bf16[32,16,256]{2,1,0:T(8,128)(2,1)S(1)}, u32[]{:S(2)}) copy-start(bf16[32,16,256]{2,1,0:T(8,128)(2,1)S(1)} %scatter_fusion) | copy-start | bytes 786436
Sparse Core Ops, SparseCore 0:
  48.3 27.6 reduce-scatter.9
  79.8 86.6 all-gather.3
  308.3 83.7 reduce-scatter.11
  401.5 70.2 reduce-scatter.7
